TPU v7x, 32 devices: a whole 2x2x4 slice. The times are simulated.
32 devices in a mesh: rows: 8 (over z, y), group: 4 (over x, core).
Axes of the slice: x: 2, y: 2, z: 4, core: 2. Of those that a mesh axis runs over, the one named last changes fastest.
Arguments:
- inputs: bfloat16 [32, 2048, 768], P('rows', 'group'), may hold values from -6 to 6
- lengths: int32 [32, 4], P('rows'), may hold values from 1 to 1024, 2048 in all within a row
- params: float32 [6, 768], replicated
- first_moment: float32 [6, 768], replicated, may hold values from -0.0234375 to 0.0234375
- second_moment: float32 [6, 768], replicated, may hold values from 1.08506946e-07 to 8.6805557e-07
- cotangent: bfloat16 [32, 1024, 768], P('rows', 'group')
Outputs:
- output: bfloat16 [32, 1024, 768], P('rows', 'group')
- grad_inputs: bfloat16 [32, 2048, 768], P('rows', 'group')
- grad_norm: float32 [], replicated
- new_params: float32 [6, 768], replicated
- new_first: float32 [6, 768], replicated
- new_second: float32 [6, 768], replicated
Inputs may be any that keep to these rules, and one draw needn't show every extreme that they name: Each row's 4 lengths sum to 2048.
All inputs are finite; a program needn't handle non-finite values.
Results may differ from a plain program's by a relative error of at most 0.0005.
Values may be sent and summed in bfloat16 or wider, within the bound.
No kernel may reach another device: no remote copies, remote signals or barrier semaphores. Data moves between devices by JAX's collectives and lax.ppermute only.
A program may use at most 256 MiB of HBM per device.

v0:
```python
import jax
import jax.numpy as jnp
from jax import lax
from jax.sharding import PartitionSpec as P

STEP = 10
beta_one = 0.9
beta_two = 0.999
learn_rate = 0.2
decay_rate = 0.01
adam_eps = 1e-08
clip_limit = 1.0


def passed_along(value, axis, steps):
    count = lax.axis_size(axis)
    initial, last = (max(0, -steps), min(count, count - steps))
    return lax.ppermute(value, axis, [(source, source + steps) for source in range(initial, last)])


def offsets(row_lengths, positions):
    seg_ends = jnp.cumsum(row_lengths)
    seg_starts = seg_ends - row_lengths
    inside = (positions[:, None] >= seg_starts[None, :]) & (positions[:, None] < seg_ends[None, :])
    chosen_start = jnp.sum(jnp.where(inside, seg_starts[None, :], 0), axis=1)
    chosen_end = jnp.sum(jnp.where(inside, seg_ends[None, :], 0), axis=1)
    return (positions - chosen_start, chosen_end - positions)


def mix_window(padded, off_ext, rem_ext, weights):
    span = padded.shape[0] - 9
    conv_rows = span + 6
    off_conv = off_ext[3 : 3 + conv_rows]
    conv_out = jnp.zeros((conv_rows, padded.shape[1]), padded.dtype) + weights[4]
    for k in range(4):
        keep_mask = (off_conv >= k).astype(padded.dtype)[:, None]
        conv_out = conv_out + keep_mask * weights[k] * padded[3 - k : 3 - k + conv_rows]
    off_own = off_ext[6 : 6 + span]
    rem_own = rem_ext[6 : 6 + span]
    pooled = []
    for block_size in range(1, 5):
        within = off_own % block_size
        upper = jnp.minimum(block_size - within, rem_own)
        count = jnp.maximum(within + upper, 1)
        running = jnp.zeros((span, padded.shape[1]), padded.dtype)
        for j in range(1 - block_size, block_size):
            keep_mask = ((j >= -within) & (j < upper)).astype(padded.dtype)[:, None]
            running = running + keep_mask * conv_out[3 + j : 3 + j + span]
        pooled.append(running / count.astype(padded.dtype)[:, None])
    stacked = jnp.stack(pooled)
    logits = jnp.sum(stacked * weights[5], axis=2)
    largest = jnp.max(logits, axis=0, keepdims=True)
    shares = jnp.exp(logits - largest)
    shares = shares / jnp.sum(shares, axis=0, keepdims=True)
    mixed = jnp.sum(shares[:, :, None] * stacked, axis=0)
    return jnp.mean(mixed.reshape(span // 2, 2, padded.shape[1]), axis=1)


def window_info(lengths, first_position, window_rows):
    positions = lax.iota(jnp.int32, window_rows) + first_position
    return jax.vmap(lambda row_lengths: offsets(row_lengths, positions))(lengths)


def apply_rows(values, info, weights):
    return jax.vmap(
        lambda row_values, row_off, row_rem: mix_window(row_values, row_off, row_rem, weights)
    )(values, info[0], info[1])


def adam_update(grads, weights, first_old, second_old):
    first_new = beta_one * first_old + (1.0 - beta_one) * grads
    second_new = beta_two * second_old + (1.0 - beta_two) * grads * grads
    first_hat = first_new / (1.0 - beta_one**STEP)
    second_hat = second_new / (1.0 - beta_two**STEP)
    updated = weights - learn_rate * (
        first_hat / (jnp.sqrt(second_hat) + adam_eps) + decay_rate * weights
    )
    return (updated, first_new, second_new)


def per_device(inputs, lengths, params, first_moment, second_moment, cotangent):
    rows_here, length_here, features = inputs.shape
    cot_rows = cotangent.shape[1]
    before_rows, after_rows, cot_before, cot_after = (6, 3, 0, 0)
    send_up = jnp.concatenate(
        [inputs[:, length_here - before_rows :], cotangent[:, cot_rows - cot_before :]], axis=1
    )
    from_below = passed_along(send_up, "group", 1)
    send_down = jnp.concatenate([inputs[:, :after_rows], cotangent[:, :cot_after]], axis=1)
    from_above = passed_along(send_down, "group", -1)
    group_start = lax.axis_index("group") * length_here
    padded = jnp.concatenate([from_below, inputs, from_above], axis=1).astype(jnp.float32)
    main_info = window_info(lengths, group_start - 6, length_here + 9)

    def forward(values, weights):
        return apply_rows(values, main_info, weights)

    output, pullback = jax.vjp(forward, padded, params)
    grad_padded, grad_local = pullback(cotangent.astype(jnp.float32))
    grad_values = grad_padded[:, 6 : 6 + length_here]
    returned_low = passed_along(grad_padded[:, :6].astype(jnp.bfloat16), "group", -1).astype(
        jnp.float32
    )
    returned_high = passed_along(
        grad_padded[:, 6 + length_here :].astype(jnp.bfloat16), "group", 1
    ).astype(jnp.float32)
    grad_values = grad_values + jnp.concatenate(
        [jnp.zeros((rows_here, length_here - 6, features), jnp.float32), returned_low], axis=1
    )
    grad_values = grad_values + jnp.concatenate(
        [returned_high, jnp.zeros((rows_here, length_here - 3, features), jnp.float32)], axis=1
    )
    grad_params = lax.psum(grad_local, ("rows", "group"))
    grad_norm = jnp.sqrt(jnp.sum(grad_params * grad_params))
    clip_scale = jnp.minimum(1.0, clip_limit / (grad_norm + 1e-06))
    new_params, new_first, new_second = adam_update(
        grad_params * clip_scale, params, first_moment, second_moment
    )
    return (
        output.astype(jnp.bfloat16),
        grad_values.astype(jnp.bfloat16),
        grad_norm,
        new_params,
        new_first,
        new_second,
    )


def solution(mesh):
    in_specs = (P("rows", "group", None), P("rows", None), P(), P(), P(), P("rows", "group", None))
    out_specs = (P("rows", "group", None), P("rows", "group", None), P(), P(), P(), P())
    return jax.shard_map(
        per_device, mesh=mesh, in_specs=in_specs, out_specs=out_specs, check_vma=False
    )
```

profile of v0, /device:TPU:1, one launch (start us, length us, event | category | flops | bytes accessed | tf_op | source)
XLA Modules:
  0.0 251.8 jit_solution(8609651600042316704)
XLA Ops:
  0.6 0.8 slice.91
  1.4 2.0 collective-permute-start.1
  3.4 0.8 slice.90
  4.2 4.5 %collective-permute-start = (bf16[4,6,768]{2,1,0:T(8,128)(2,1)S(1)}, bf16[4,6,768]{2,1,0:T(8,128)(2,1)S(1)}, u32[]{:S(2)}, u32[]{:S(2)}) collective-permute-start(bf16[4,6,768]{2,1,0:T(8,128)(2,1)S(1)} %slice.90), channel_id=1, source_target_pairs={{0,1},{1,2},{2,3},{4,5},{5,6},{6,7},{8,9},{9,10},{10,11},{12,13},{... | collective-permute-start | bytes 110600 | tf_op jit(solution)/shard_map/ppermute | solution.py:18
  8.7 0.9 reduce_window_sum.11
  9.6 0.7 sub.50
  10.3 0.1 slice.112
  10.3 0.1 select_reduce_fusion.1
  10.5 0.1 compare_convert_fusion.3
  10.6 0.1 compare_convert_fusion.4
  10.6 0.1 and_convert_fusion.14
  10.7 0.1 maximum_convert_fusion.3
  10.8 0.1 and_convert_fusion.13
  11.0 1.7 convert_multiply_fusion
  12.7 1.0 slice_reduce_fusion.5
  13.7 4.7 %broadcast_in_dim.41 = f32[4,256,2,768]{3,2,1,0:T(2,128)} broadcast(f32[4,256,768]{2,1,0:T(8,128)S(1)} %convert_multiply_fusion), dimensions={0,1,3} | broadcast | bytes 9437184 | tf_op jit(solution)/shard_map/transpose(jvp(vmap()))/broadcast_in_dim | solution.py:56
  18.3 8.7 %reshape.120 = f32[4,512,768]{2,1,0:T(8,128)} reshape(f32[4,256,2,768]{3,2,1,0:T(2,128)} %broadcast_in_dim.41) | data formatting | bytes 12582912 | tf_op jit(solution)/shard_map/transpose(jvp(vmap()))/reshape | solution.py:56
  27.0 0.0 collective-permute-done.1
  27.0 0.0 collective-permute-done
  27.0 0.0 copy-done.4
  27.0 0.7 maximum_convert_fusion
  27.7 0.0 copy-start
  27.7 4.8 %fusion.3 = f32[4,518,768]{2,1,0:T(8,128)S(1)} fusion(f32[4,521,768]{2,1,0:T(8,128)S(1)} %maximum_convert_fusion, f32[768]{0:T(1024)S(1)} %get-tuple-element.16, f32[4,518]{1,0:T(4,128)S(1)} %get-tuple-element.86, f32[768]{0:T(1024)S(1)} %get-tuple-element.17, f32[4,518]{1,0:T(4,128)S(1)} %get-tuple-element.85, f32[768]{0:T(1024)S(1)} %get-tuple-element.18, ...), kind=kLoop, calls=%fused_computation.18 | loop fusion | flops 19095552 | bytes 31874432 | tf_op jit(solution)/shard_map/jvp(vmap())/add | solution.py:37
  32.6 6.4 %divide_bitcast_fusion.1 = (f32[1,4,512,768]{3,2,1,0:T(8,128)S(1)}, f32[1,4,512,768]{3,2,1,0:T(8,128)S(1)}) fusion(f32[4,518,768]{2,1,0:T(8,128)S(1)} %fusion.3, f32[4,512]{1,0:T(4,128)S(1)} %get-tuple-element.75, f32[4,512]{1,0:T(4,128)S(1)} %get-tuple-element.72, f32[4,512]{1,0:T(4,128)S(1)} %get-tuple-element.66, f32[4,512]{1,0:T(4,128)S(1)} %get-tuple-element.35, ...), kind=kLoop, calls=%fused_computation.48 | loop fusion | flops 25165824 | bytes 44122112 | tf_op jit(solution)/shard_map/jvp(vmap())/stack | solution.py:50
  39.0 8.8 %divide_bitcast_fusion.2 = (f32[1,4,512,768]{3,2,1,0:T(8,128)S(1)}, f32[1,4,512,768]{3,2,1,0:T(8,128)}) fusion(f32[4,518,768]{2,1,0:T(8,128)S(1)} %fusion.3, f32[4,512]{1,0:T(4,128)S(1)} %get-tuple-element.87, f32[4,512]{1,0:T(4,128)S(1)} %get-tuple-element.33, f32[4,512]{1,0:T(4,128)S(1)} %get-tuple-element.76, f32[4,512]{1,0:T(4,128)S(1)} %get-tuple-element.71, ...), kind=kLoop, calls=%fused_computation.49 | loop fusion | flops 25165824 | bytes 56705024 | tf_op jit(solution)/shard_map/jvp(vmap())/stack | solution.py:50
  47.8 17.0 %multiply_reduce_fusion.1 = (f32[4,4,512]{2,0,1:T(4,128)S(1)}, f32[4,4,512]{2,0,1:T(4,128)S(1)}) fusion(f32[4,512,768]{2,1,0:T(8,128)} %reshape.120, f32[1,4,512,768]{3,2,1,0:T(8,128)} %get-tuple-element.61, f32[1,4,512,768]{3,2,1,0:T(8,128)S(1)} %get-tuple-element.63, f32[1,4,512,768]{3,2,1,0:T(8,128)S(1)} %get-tuple-element.62, ...), kind=kLoop, calls=%fused_computation.3 | loop fusion | flops 44023808 | bytes 31525888 | tf_op jit(solution)/shard_map/transpose(jvp(vmap()))/reduce_sum | solution.py:55
  64.8 0.0 copy-done.3
  65.0 14.1 %multiply_reduce_fusion = (f32[768]{0:T(1024)S(1)}, f32[4,512,768]{2,1,0:T(8,128)}) fusion(f32[4,4,512]{2,0,1:T(4,128)S(1)} %select_add_fusion, f32[1,4,512,768]{3,2,1,0:T(8,128)} %get-tuple-element.61, f32[1,4,512,768]{3,2,1,0:T(8,128)} %copy-done.2, f32[1,4,512,768]{3,2,1,0:T(8,128)} %copy-done.1, f32[1,4,512,768]{3,2,1,0:T(8,128)} %copy-done.3, ...), kind=kLoop, calls=%fused_computation.1 | loop fusion | flops 42466560 | bytes 31525888 | tf_op jit(solution)/shard_map/transpose(jvp(vmap()))/reduce_sum | solution.py:51
  79.2 11.4 %multiply_add_fusion = f32[4,4,512,768]{3,2,0,1:T(8,128)} fusion(f32[4,4,512]{2,0,1:T(4,128)S(1)} %copy.31, f32[4,512,768]{2,1,0:T(8,128)} %reshape.120, f32[4,4,512]{2,0,1:T(4,128)S(1)} %copy.30, f32[768]{0:T(1024)S(1)} %get-tuple-element.20), kind=kLoop, calls=%fused_computation.2 | loop fusion | flops 18874368 | bytes 31525888 | tf_op jit(solution)/shard_map/transpose(jvp(vmap()))/add_any | solution.py:51
  90.6 20.8 %broadcast_multiply_fusion.7 = (f32[4,512,768]{2,1,0:T(8,128)}, f32[4,512,768]{2,1,0:T(8,128)}, f32[4,512,768]{2,1,0:T(8,128)}, f32[4,512,768]{2,1,0:T(8,128)}, ...) fusion(f32[4,512]{1,0:T(4,128)S(1)} %get-tuple-element.80, ...), kind=kLoop, calls=%fused_computation.61 | loop fusion | flops 15728640 | bytes 62996480 | tf_op jit(solution)/shard_map/transpose(jvp(vmap()))/mul | solution.py:48
  111.3 20.6 %broadcast_multiply_fusion = (f32[4,512,768]{2,1,0:T(8,128)}, f32[4,512,768]{2,1,0:T(8,128)}, f32[4,512,768]{2,1,0:T(8,128)}, f32[4,512,768]{2,1,0:T(8,128)}, f3...) fusion(f32[4,512]{1,0:T(4,128)S(1)} %get-tuple-element.71, ...), kind=kLoop, calls=%fused_computation.54 | loop fusion | flops 15728640 | bytes 62996480 | tf_op jit(solution)/shard_map/transpose(jvp(vmap()))/mul | solution.py:48
  131.9 36.3 %multiply_reduce_fusion.7 = (f32[768]{0:T(1024)S(1)}, f32[768]{0:T(1024)S(1)}, f32[768]{0:T(1024)S(1)}, f32[768]{0:T(1024)S(1)}, f32[768]{0:T(1024)S(1)}, /*index=5*/f32[4,518,768]{2,1,0:T(8,128)}) fusion(f32[4,521,768]{2,1,0:T(8,128)S(1)} %bitcast.77, f32[4,518]{1,0:T(4,128)S(1)} %get-tuple-element.86, f32[4,518]{1,0:T(4,128)S(1)} %get-tuple-element.83, ...), kind=kLoop, calls=%fused_computation.22 | loop fusion | flops 44552448 | bytes 132537728 | tf_op jit(solution)/shard_map/transpose(jvp(vmap()))/reduce_sum | solution.py:37
  168.2 7.7 %multiply_multiply_fusion = (f32[4,518,768]{2,1,0:T(8,128)S(1)}, f32[4,518,768]{2,1,0:T(8,128)S(1)}, f32[4,518,768]{2,1,0:T(8,128)S(1)}, f32[4,518,768]{2,1,0:T(8,128)}) fusion(f32[4,518,768]{2,1,0:T(8,128)} %get-tuple-element.26, f32[768]{0:T(1024)S(1)} %get-tuple-element.16, f32[4,518]{1,0:T(4,128)S(1)} %get-tuple-element.86, ...), kind=kLoop, calls=%fused_computation.6 | loop fusion | flops 12730368 | bytes 31871360 | tf_op jit(solution)/shard_map/transpose(jvp(vmap()))/mul | solution.py:37
  175.9 6.8 %fusion.23 = (bf16[4,521,768]{2,1,0:T(8,128)(2,1)}, f32[4,521,768]{2,1,0:T(8,128)}) fusion(f32[4,518,768]{2,1,0:T(8,128)S(1)} %get-tuple-element.57, f32[4,518,768]{2,1,0:T(8,128)S(1)} %get-tuple-element.58, f32[4,518,768]{2,1,0:T(8,128)} %get-tuple-element.59, f32[4,518,768]{2,1,0:T(8,128)S(1)} %get-tuple-element.56), kind=kLoop, calls=%fused_computation.131 | loop fusion | flops 6402048 | bytes 35063808 | tf_op jit(solution)/shard_map/convert.5
  182.7 0.9 slice.128
  183.6 0.8 slice.127
  184.4 0.0 copy-start.6
  184.4 0.0 copy-start.7
  184.4 8.7 %bitcast_reduce_fusion = f32[4,256,768]{2,0,1:T(4,128)S(1)} fusion(f32[4,512,768]{2,1,0:T(8,128)} %get-tuple-element.7), kind=kLoop, calls=%fused_computation.46 | loop fusion | flops 786432 | bytes 9437184 | tf_op jit(solution)/shard_map/jvp(vmap())/reduce_sum | solution.py:56
  193.1 1.7 fusion.19
  194.9 38.8 %psum.7 = f32[6,768]{1,0:T(8,128)S(1)} all-reduce(f32[6,768]{1,0:T(8,128)S(1)} %pad_add_fusion.2), channel_id=1, replica_groups=mesh['rows'=8,'group'=4] {'rows','group'}, use_global_device_ids=true, to_apply=%region_18.19 | all-reduce | flops 4608 | bytes 36864 | tf_op jit(solution)/shard_map/psum | solution.py:113
  233.6 0.6 multiply_reduce_fusion.9
  235.0 5.2 %collective-permute-start.3 = (bf16[4,3,768]{2,1,0:T(4,128)(2,1)S(1)}, bf16[4,3,768]{2,1,0:T(4,128)(2,1)S(1)}, u32[]{:S(2)}, u32[]{:S(2)}) collective-permute-start(bf16[4,3,768]{2,1,0:T(4,128)(2,1)S(1)} %slice.128), channel_id=1, source_target_pairs={{0,1},{1,2},{2,3},{4,5},{5,6},{6,7},{8,9},{9,10},{10,11},{12,13},{... | collective-permute-start | bytes 55304 | tf_op jit(solution)/shard_map/ppermute | solution.py:18
  240.2 1.9 collective-permute-start.2
  242.1 0.6 multiply_subtract_fusion
  242.8 0.0 collective-permute-done.3
  242.8 2.8 %collective-permute-done.2 = bf16[4,6,768]{2,1,0:T(8,128)(2,1)S(1)} collective-permute-done((bf16[4,6,768]{2,1,0:T(8,128)(2,1)S(1)}, bf16[4,6,768]{2,1,0:T(8,128)(2,1)S(1)}, u32[]{:S(2)}, u32[]{:S(2)}) %collective-permute-start.2) | collective-permute-done | bytes 36896 | tf_op jit(solution)/shard_map/ppermute | solution.py:18
  245.6 5.1 %fusion.5 = bf16[4,512,768]{2,1,0:T(8,128)(2,1)} fusion(f32[4,521,768]{2,1,0:T(8,128)} %get-tuple-element.28, bf16[4,3,768]{2,1,0:T(4,128)(2,1)S(1)} %collective-permute-done.3, bf16[4,6,768]{2,1,0:T(8,128)(2,1)S(1)} %collective-permute-done.2), kind=kLoop, calls=%fused_computation.26 | loop fusion | flops 7864320 | bytes 9492480 | tf_op jit(solution)/shard_map/convert_element_type | solution.py:121
  (35 shorter events, 0.3 us)
Async XLA Ops:
  1.4 25.6 %collective-permute-start.1 = (bf16[4,3,768]{2,1,0:T(4,128)(2,1)S(1)}, bf16[4,3,768]{2,1,0:T(4,128)(2,1)S(1)}, u32[]{:S(2)}, u32[]{:S(2)}) collective-permute-start(bf16[4,3,768]{2,1,0:T(4,128)(2,1)S(1)} %slice.91), channel_id=1, source_target_pairs={{1,0},{2,1},{3,2},{5,4},{6,5},{7,6},{9,8},{10,9},{11,10},{13,12},{... | collective-permute-start | bytes 55304 | tf_op jit(solution)/shard_map/ppermute | solution.py:18
  4.2 22.8 %collective-permute-start = (bf16[4,6,768]{2,1,0:T(8,128)(2,1)S(1)}, bf16[4,6,768]{2,1,0:T(8,128)(2,1)S(1)}, u32[]{:S(2)}, u32[]{:S(2)}) collective-permute-start(bf16[4,6,768]{2,1,0:T(8,128)(2,1)S(1)} %slice.90), channel_id=1, source_target_pairs={{0,1},{1,2},{2,3},{4,5},{5,6},{6,7},{8,9},{9,10},{10,11},{12,13},{... | collective-permute-start | bytes 110600 | tf_op jit(solution)/shard_map/ppermute | solution.py:18
  18.3 8.7 %copy-start.4 = (bf16[4,512,768]{2,1,0:T(8,128)(2,1)S(1)}, bf16[4,512,768]{2,1,0:T(8,128)(2,1)}, u32[]{:S(2)}) copy-start(bf16[4,512,768]{2,1,0:T(8,128)(2,1)} %param.6) | copy-start | bytes 9437188
  27.7 4.9 %copy-start = (f32[4,521,768]{2,1,0:T(8,128)}, f32[4,521,768]{2,1,0:T(8,128)S(1)}, u32[]{:S(2)}) copy-start(f32[4,521,768]{2,1,0:T(8,128)S(1)} %maximum_convert_fusion) | copy-start | bytes 19206148
  39.0 8.8 %copy-start.1 = (f32[1,4,512,768]{3,2,1,0:T(8,128)}, f32[1,4,512,768]{3,2,1,0:T(8,128)S(1)}, u32[]{:S(2)}) copy-start(f32[1,4,512,768]{3,2,1,0:T(8,128)S(1)} %get-tuple-element.62) | copy-start | bytes 18874372
  39.0 8.8 %copy-start.2 = (f32[1,4,512,768]{3,2,1,0:T(8,128)}, f32[1,4,512,768]{3,2,1,0:T(8,128)S(1)}, u32[]{:S(2)}) copy-start(f32[1,4,512,768]{3,2,1,0:T(8,128)S(1)} %get-tuple-element.63) | copy-start | bytes 18874372
  47.8 17.0 %copy-start.3 = (f32[1,4,512,768]{3,2,1,0:T(8,128)}, f32[1,4,512,768]{3,2,1,0:T(8,128)S(1)}, u32[]{:S(2)}) copy-start(f32[1,4,512,768]{3,2,1,0:T(8,128)S(1)} %get-tuple-element.60) | copy-start | bytes 18874372
  90.6 41.3 %slice-start = ((s8[6488064]{0:T(1024)(128)(4,1)}), s8[4194304]{0:T(1024)(128)(4,1)S(1)}, s32[]{:S(2)}) async-start(s8[6488064]{0:T(1024)(128)(4,1)} %bitcast.76), calls=%async_computation | async-start | bytes 8388608
  111.3 20.6 %slice-start.1 = ((s8[6488064]{0:T(1024)(128)(4,1)}), s8[2293760]{0:T(1024)(128)(4,1)S(1)}, s32[]{:S(2)}) async-start(s8[6488064]{0:T(1024)(128)(4,1)} %bitcast.76), calls=%async_computation.1 | async-start | bytes 4587520
  184.4 57.7 %copy-start.5 = (f32[6,768]{1,0:T(8,128)S(1)}, f32[6,768]{1,0:T(8,128)}, u32[]{:S(2)}) copy-start(f32[6,768]{1,0:T(8,128)} %param.8) | copy-start | bytes 55300
  184.4 57.7 %copy-start.6 = (f32[6,768]{1,0:T(8,128)S(1)}, f32[6,768]{1,0:T(8,128)}, u32[]{:S(2)}) copy-start(f32[6,768]{1,0:T(8,128)} %param.9) | copy-start | bytes 55300
  184.4 57.7 %copy-start.7 = (f32[6,768]{1,0:T(8,128)S(1)}, f32[6,768]{1,0:T(8,128)}, u32[]{:S(2)}) copy-start(f32[6,768]{1,0:T(8,128)} %param.10) | copy-start | bytes 55300
  235.0 7.8 %collective-permute-start.3 = (bf16[4,3,768]{2,1,0:T(4,128)(2,1)S(1)}, bf16[4,3,768]{2,1,0:T(4,128)(2,1)S(1)}, u32[]{:S(2)}, u32[]{:S(2)}) collective-permute-start(bf16[4,3,768]{2,1,0:T(4,128)(2,1)S(1)} %slice.128), channel_id=1, source_target_pairs={{0,1},{1,2},{2,3},{4,5},{5,6},{6,7},{8,9},{9,10},{10,11},{12,13},{... | collective-permute-start | bytes 55304 | tf_op jit(solution)/shard_map/ppermute | solution.py:18
  240.2 5.4 %collective-permute-start.2 = (bf16[4,6,768]{2,1,0:T(8,128)(2,1)S(1)}, bf16[4,6,768]{2,1,0:T(8,128)(2,1)S(1)}, u32[]{:S(2)}, u32[]{:S(2)}) collective-permute-start(bf16[4,6,768]{2,1,0:T(8,128)(2,1)S(1)} %slice.127), channel_id=1, source_target_pairs={{1,0},{2,1},{3,2},{5,4},{6,5},{7,6},{9,8},{10,9},{11,10},{13,12},{... | collective-permute-start | bytes 110600 | tf_op jit(solution)/shard_map/ppermute | solution.py:18
where the time goes:
time: 253 us; the launch traced here: 252 us
  other arithmetic  176 us (70%)
  blocking collectives  38.8 us (15%)
  local copies, waits for them, and re-layouts  17.9 us (7%)
  starting transfers between devices  13.6 us (5%)
  waiting for transfers between devices  2.81 us (1%)
  between operations  2.81 us (1%)
    mul x2, other arithmetic, mix_window(): running = running + keep_mask * conv_out[3 + j:3 + j + span]  41.3 us
    psum x1, blocking collectives, per_device(): grad_params = lax.psum(grad_local, ('rows', 'group'))  38.8 us
    reduce_sum x1, other arithmetic, mix_window(): keep_mask * weights[k] * padded[3 - k:3 - k + conv_rows]  36.3 us
    reduce_sum x1, other arithmetic, mix_window(): mixed = jnp.sum(shares[:, :, None] * stacked, axis=0)  17 us
    another operation x2, other arithmetic, mix_window(): stacked = jnp.stack(pooled)  15.2 us
    reduce_sum x1, other arithmetic, mix_window(): logits = jnp.sum(stacked * weights[5], axis=2)  14.1 us
    ppermute x4, starting transfers between devices, passed_along(): lax.ppermute(value, axis, [(source, source + steps) for source in range(i...  13.6 us
    add_any x1, other arithmetic, mix_window(): logits = jnp.sum(stacked * weights[5], axis=2)  11.4 us
  transfers between devices with their start and end apart: 4, of which 1 were waited for; matrix products, arithmetic and copies ran while one was open for 8% of the time, Pallas kernels for 0%

commit v1 on v0

--- a/solution.py
+++ b/solution.py
@@ -10,6 +10,11 @@
 decay_rate = 0.01
 adam_eps = 1e-08
 clip_limit = 1.0
+
+
+def add_all(x, mesh_axis):
+    shards = lax.all_gather(x, mesh_axis)
+    return jnp.sum(shards, axis=0)
 
 
 def passed_along(value, axis, steps):
@@ -110,7 +115,7 @@
     grad_values = grad_values + jnp.concatenate(
         [returned_high, jnp.zeros((rows_here, length_here - 3, features), jnp.float32)], axis=1
     )
-    grad_params = lax.psum(grad_local, ("rows", "group"))
+    grad_params = add_all(grad_local, ("rows", "group"))
     grad_norm = jnp.sqrt(jnp.sum(grad_params * grad_params))
     clip_scale = jnp.minimum(1.0, clip_limit / (grad_norm + 1e-06))
     new_params, new_first, new_second = adam_update(

time: 253 us -> 254 us (level)
  blocking collectives: 38.8 us -> 43.2 us
  starting transfers between devices: 13.6 us -> 10.8 us
    all_gather x0 -> x1, blocking collectives: none -> 43.2 us  [add_all(): shards = lax.all_gather(x, mesh_axis)]
    psum x1 -> x0, blocking collectives: 38.8 us -> none  [per_device(): grad_params = lax.psum(grad_local, ('rows', 'group'))]
    ppermute x4, starting transfers between devices: 13.6 us -> 10.8 us  [passed_along(): lax.ppermute(value, axis, [(source, source + steps) for source in range(i...]
where the time goes in v1:
time: 254 us; the launch traced here: 253 us
  other arithmetic  176 us (69%)
  blocking collectives  43.2 us (17%)
  local copies, waits for them, and re-layouts  17.9 us (7%)
  starting transfers between devices  10.8 us (4%)
  between operations  2.8 us (1%)
    all_gather x1, blocking collectives, add_all(): shards = lax.all_gather(x, mesh_axis)  43.2 us
    mul x2, other arithmetic, mix_window(): running = running + keep_mask * conv_out[3 + j:3 + j + span]  41.3 us
    reduce_sum x1, other arithmetic, mix_window(): keep_mask * weights[k] * padded[3 - k:3 - k + conv_rows]  36.3 us
    reduce_sum x1, other arithmetic, mix_window(): mixed = jnp.sum(shares[:, :, None] * stacked, axis=0)  17 us
    another operation x2, other arithmetic, mix_window(): stacked = jnp.stack(pooled)  15.2 us
    reduce_sum x1, other arithmetic, mix_window(): logits = jnp.sum(stacked * weights[5], axis=2)  14.1 us
    add_any x1, other arithmetic, mix_window(): logits = jnp.sum(stacked * weights[5], axis=2)  11.4 us
    ppermute x4, starting transfers between devices, passed_along(): lax.ppermute(value, axis, [(source, source + steps) for source in range(i...  10.8 us
  transfers between devices with their start and end apart: 4, of which 1 were waited for; matrix products, arithmetic and copies ran while one was open for 8% of the time, Pallas kernels for 0%

profile of v1, /device:TPU:1, one launch (start us, length us, event | category | flops | bytes accessed | tf_op | source)
XLA Modules:
  0.0 253.0 jit_solution(11094021499103009145)
XLA Ops:
  0.6 0.8 slice.91
  1.4 2.0 collective-permute-start.1
  3.4 0.8 slice.90
  4.2 4.5 %collective-permute-start = (bf16[4,6,768]{2,1,0:T(8,128)(2,1)S(1)}, bf16[4,6,768]{2,1,0:T(8,128)(2,1)S(1)}, u32[]{:S(2)}, u32[]{:S(2)}) collective-permute-start(bf16[4,6,768]{2,1,0:T(8,128)(2,1)S(1)} %slice.90), channel_id=1, source_target_pairs={{0,1},{1,2},{2,3},{4,5},{5,6},{6,7},{8,9},{9,10},{10,11},{12,13},{... | collective-permute-start | bytes 110600 | tf_op jit(solution)/shard_map/ppermute | solution.py:23
  8.7 0.9 reduce_window_sum.11
  9.6 0.7 sub.50
  10.3 0.1 slice.112
  10.3 0.1 select_reduce_fusion.1
  10.5 0.1 compare_convert_fusion.3
  10.6 0.1 compare_convert_fusion.4
  10.6 0.1 and_convert_fusion.14
  10.7 0.1 maximum_convert_fusion.3
  10.8 0.1 and_convert_fusion.13
  11.0 1.7 convert_multiply_fusion
  12.7 1.0 slice_reduce_fusion.5
  13.7 4.7 %broadcast_in_dim.41 = f32[4,256,2,768]{3,2,1,0:T(2,128)} broadcast(f32[4,256,768]{2,1,0:T(8,128)S(1)} %convert_multiply_fusion), dimensions={0,1,3} | broadcast | bytes 9437184 | tf_op jit(solution)/shard_map/transpose(jvp(vmap()))/broadcast_in_dim | solution.py:61
  18.3 8.7 %reshape.120 = f32[4,512,768]{2,1,0:T(8,128)} reshape(f32[4,256,2,768]{3,2,1,0:T(2,128)} %broadcast_in_dim.41) | data formatting | bytes 12582912 | tf_op jit(solution)/shard_map/transpose(jvp(vmap()))/reshape | solution.py:61
  27.0 0.0 collective-permute-done.1
  27.0 0.0 collective-permute-done
  27.0 0.0 copy-done.4
  27.0 0.7 maximum_convert_fusion
  27.7 4.8 %fusion.3 = f32[4,518,768]{2,1,0:T(8,128)S(1)} fusion(f32[4,521,768]{2,1,0:T(8,128)S(1)} %maximum_convert_fusion, f32[768]{0:T(1024)S(1)} %get-tuple-element.16, f32[4,518]{1,0:T(4,128)S(1)} %get-tuple-element.86, f32[768]{0:T(1024)S(1)} %get-tuple-element.17, f32[4,518]{1,0:T(4,128)S(1)} %get-tuple-element.85, f32[768]{0:T(1024)S(1)} %get-tuple-element.18, ...), kind=kLoop, calls=%fused_computation.18 | loop fusion | flops 19095552 | bytes 31874432 | tf_op jit(solution)/shard_map/jvp(vmap())/add | solution.py:42
  32.6 6.4 %divide_bitcast_fusion.1 = (f32[1,4,512,768]{3,2,1,0:T(8,128)S(1)}, f32[1,4,512,768]{3,2,1,0:T(8,128)S(1)}) fusion(f32[4,518,768]{2,1,0:T(8,128)S(1)} %fusion.3, f32[4,512]{1,0:T(4,128)S(1)} %get-tuple-element.75, f32[4,512]{1,0:T(4,128)S(1)} %get-tuple-element.72, f32[4,512]{1,0:T(4,128)S(1)} %get-tuple-element.66, f32[4,512]{1,0:T(4,128)S(1)} %get-tuple-element.35, ...), kind=kLoop, calls=%fused_computation.48 | loop fusion | flops 25165824 | bytes 44122112 | tf_op jit(solution)/shard_map/jvp(vmap())/stack | solution.py:55
  39.0 8.8 %divide_bitcast_fusion.2 = (f32[1,4,512,768]{3,2,1,0:T(8,128)S(1)}, f32[1,4,512,768]{3,2,1,0:T(8,128)}) fusion(f32[4,518,768]{2,1,0:T(8,128)S(1)} %fusion.3, f32[4,512]{1,0:T(4,128)S(1)} %get-tuple-element.87, f32[4,512]{1,0:T(4,128)S(1)} %get-tuple-element.33, f32[4,512]{1,0:T(4,128)S(1)} %get-tuple-element.76, f32[4,512]{1,0:T(4,128)S(1)} %get-tuple-element.71, ...), kind=kLoop, calls=%fused_computation.49 | loop fusion | flops 25165824 | bytes 56705024 | tf_op jit(solution)/shard_map/jvp(vmap())/stack | solution.py:55
  47.8 17.0 %multiply_reduce_fusion.1 = (f32[4,4,512]{2,0,1:T(4,128)S(1)}, f32[4,4,512]{2,0,1:T(4,128)S(1)}) fusion(f32[4,512,768]{2,1,0:T(8,128)} %reshape.120, f32[1,4,512,768]{3,2,1,0:T(8,128)} %get-tuple-element.61, f32[1,4,512,768]{3,2,1,0:T(8,128)S(1)} %get-tuple-element.63, f32[1,4,512,768]{3,2,1,0:T(8,128)S(1)} %get-tuple-element.62, ...), kind=kLoop, calls=%fused_computation.3 | loop fusion | flops 44023808 | bytes 31525888 | tf_op jit(solution)/shard_map/transpose(jvp(vmap()))/reduce_sum | solution.py:60
  64.8 0.0 copy-done.3
  65.0 14.1 %multiply_reduce_fusion = (f32[768]{0:T(1024)S(1)}, f32[4,512,768]{2,1,0:T(8,128)}) fusion(f32[4,4,512]{2,0,1:T(4,128)S(1)} %select_add_fusion, f32[1,4,512,768]{3,2,1,0:T(8,128)} %get-tuple-element.61, f32[1,4,512,768]{3,2,1,0:T(8,128)} %copy-done.2, f32[1,4,512,768]{3,2,1,0:T(8,128)} %copy-done.1, f32[1,4,512,768]{3,2,1,0:T(8,128)} %copy-done.3, ...), kind=kLoop, calls=%fused_computation.1 | loop fusion | flops 42466560 | bytes 31525888 | tf_op jit(solution)/shard_map/transpose(jvp(vmap()))/reduce_sum | solution.py:56
  79.2 11.4 %multiply_add_fusion = f32[4,4,512,768]{3,2,0,1:T(8,128)} fusion(f32[4,4,512]{2,0,1:T(4,128)S(1)} %copy.36, f32[4,512,768]{2,1,0:T(8,128)} %reshape.120, f32[4,4,512]{2,0,1:T(4,128)S(1)} %copy.35, f32[768]{0:T(1024)S(1)} %get-tuple-element.20), kind=kLoop, calls=%fused_computation.2 | loop fusion | flops 18874368 | bytes 31525888 | tf_op jit(solution)/shard_map/transpose(jvp(vmap()))/add_any | solution.py:56
  90.6 20.8 %broadcast_multiply_fusion.7 = (f32[4,512,768]{2,1,0:T(8,128)}, f32[4,512,768]{2,1,0:T(8,128)}, f32[4,512,768]{2,1,0:T(8,128)}, f32[4,512,768]{2,1,0:T(8,128)}, ...) fusion(f32[4,512]{1,0:T(4,128)S(1)} %get-tuple-element.80, ...), kind=kLoop, calls=%fused_computation.61 | loop fusion | flops 15728640 | bytes 62996480 | tf_op jit(solution)/shard_map/transpose(jvp(vmap()))/mul | solution.py:53
  111.3 20.6 %broadcast_multiply_fusion = (f32[4,512,768]{2,1,0:T(8,128)}, f32[4,512,768]{2,1,0:T(8,128)}, f32[4,512,768]{2,1,0:T(8,128)}, f32[4,512,768]{2,1,0:T(8,128)}, f3...) fusion(f32[4,512]{1,0:T(4,128)S(1)} %get-tuple-element.71, ...), kind=kLoop, calls=%fused_computation.54 | loop fusion | flops 15728640 | bytes 62996480 | tf_op jit(solution)/shard_map/transpose(jvp(vmap()))/mul | solution.py:53
  131.9 36.3 %multiply_reduce_fusion.7 = (f32[768]{0:T(1024)S(1)}, f32[768]{0:T(1024)S(1)}, f32[768]{0:T(1024)S(1)}, f32[768]{0:T(1024)S(1)}, f32[768]{0:T(1024)S(1)}, /*index=5*/f32[4,518,768]{2,1,0:T(8,128)}) fusion(f32[4,521,768]{2,1,0:T(8,128)S(1)} %bitcast.79, f32[4,518]{1,0:T(4,128)S(1)} %get-tuple-element.86, f32[4,518]{1,0:T(4,128)S(1)} %get-tuple-element.83, ...), kind=kLoop, calls=%fused_computation.22 | loop fusion | flops 44552448 | bytes 132537728 | tf_op jit(solution)/shard_map/transpose(jvp(vmap()))/reduce_sum | solution.py:42
  168.2 7.7 %multiply_multiply_fusion = (f32[4,518,768]{2,1,0:T(8,128)S(1)}, f32[4,518,768]{2,1,0:T(8,128)S(1)}, f32[4,518,768]{2,1,0:T(8,128)S(1)}, f32[4,518,768]{2,1,0:T(8,128)}) fusion(f32[4,518,768]{2,1,0:T(8,128)} %get-tuple-element.26, f32[768]{0:T(1024)S(1)} %get-tuple-element.16, f32[4,518]{1,0:T(4,128)S(1)} %get-tuple-element.86, ...), kind=kLoop, calls=%fused_computation.6 | loop fusion | flops 12730368 | bytes 31871360 | tf_op jit(solution)/shard_map/transpose(jvp(vmap()))/mul | solution.py:42
  175.9 6.8 %fusion.23 = (bf16[4,521,768]{2,1,0:T(8,128)(2,1)}, f32[4,521,768]{2,1,0:T(8,128)}) fusion(f32[4,518,768]{2,1,0:T(8,128)S(1)} %get-tuple-element.57, f32[4,518,768]{2,1,0:T(8,128)S(1)} %get-tuple-element.58, f32[4,518,768]{2,1,0:T(8,128)} %get-tuple-element.59, f32[4,518,768]{2,1,0:T(8,128)S(1)} %get-tuple-element.56), kind=kLoop, calls=%fused_computation.131 | loop fusion | flops 6402048 | bytes 35063808 | tf_op jit(solution)/shard_map/convert.5
  182.7 0.9 slice.128
  183.6 0.8 slice.127
  184.4 0.0 copy-start.6
  184.4 0.0 copy-start.7
  184.4 8.7 %bitcast_reduce_fusion = f32[4,256,768]{2,0,1:T(4,128)S(1)} fusion(f32[4,512,768]{2,1,0:T(8,128)} %get-tuple-element.7), kind=kLoop, calls=%fused_computation.46 | loop fusion | flops 786432 | bytes 9437184 | tf_op jit(solution)/shard_map/jvp(vmap())/reduce_sum | solution.py:61
  193.1 1.7 fusion.19
  194.9 43.2 %all-gather.1 = f32[32,6,768]{2,1,0:T(8,128)S(1)} all-gather(f32[1,6,768]{2,1,0:T(8,128)S(1)} %add_bitcast_fusion), channel_id=2, replica_groups=mesh['rows'=8,'group'=4] {'rows','group'}, dimensions={0}, use_global_device_ids=true | all-gather | bytes 608256 | tf_op jit(solution)/shard_map/all_gather | solution.py:16
  238.0 0.1 reduce_sum.184
  238.1 0.6 multiply_reduce_fusion.9
  239.5 1.9 collective-permute-start.3
  241.4 2.4 collective-permute-start.2
  243.8 0.6 multiply_subtract_fusion
  244.5 0.0 collective-permute-done.3
  244.5 2.3 collective-permute-done.2
  246.8 5.1 %fusion.5 = bf16[4,512,768]{2,1,0:T(8,128)(2,1)} fusion(f32[4,521,768]{2,1,0:T(8,128)} %get-tuple-element.28, bf16[4,3,768]{2,1,0:T(4,128)(2,1)S(1)} %collective-permute-done.3, bf16[4,6,768]{2,1,0:T(8,128)(2,1)S(1)} %collective-permute-done.2), kind=kLoop, calls=%fused_computation.26 | loop fusion | flops 7864320 | bytes 9492480 | tf_op jit(solution)/shard_map/convert_element_type | solution.py:126
  (36 shorter events, 0.3 us)
Async XLA Ops:
  1.4 25.6 %collective-permute-start.1 = (bf16[4,3,768]{2,1,0:T(4,128)(2,1)S(1)}, bf16[4,3,768]{2,1,0:T(4,128)(2,1)S(1)}, u32[]{:S(2)}, u32[]{:S(2)}) collective-permute-start(bf16[4,3,768]{2,1,0:T(4,128)(2,1)S(1)} %slice.91), channel_id=1, source_target_pairs={{1,0},{2,1},{3,2},{5,4},{6,5},{7,6},{9,8},{10,9},{11,10},{13,12},{... | collective-permute-start | bytes 55304 | tf_op jit(solution)/shard_map/ppermute | solution.py:23
  4.2 22.8 %collective-permute-start = (bf16[4,6,768]{2,1,0:T(8,128)(2,1)S(1)}, bf16[4,6,768]{2,1,0:T(8,128)(2,1)S(1)}, u32[]{:S(2)}, u32[]{:S(2)}) collective-permute-start(bf16[4,6,768]{2,1,0:T(8,128)(2,1)S(1)} %slice.90), channel_id=1, source_target_pairs={{0,1},{1,2},{2,3},{4,5},{5,6},{6,7},{8,9},{9,10},{10,11},{12,13},{... | collective-permute-start | bytes 110600 | tf_op jit(solution)/shard_map/ppermute | solution.py:23
  18.3 8.7 %copy-start.4 = (bf16[4,512,768]{2,1,0:T(8,128)(2,1)S(1)}, bf16[4,512,768]{2,1,0:T(8,128)(2,1)}, u32[]{:S(2)}) copy-start(bf16[4,512,768]{2,1,0:T(8,128)(2,1)} %param.6) | copy-start | bytes 9437188
  27.7 4.9 %copy-start = (f32[4,521,768]{2,1,0:T(8,128)}, f32[4,521,768]{2,1,0:T(8,128)S(1)}, u32[]{:S(2)}) copy-start(f32[4,521,768]{2,1,0:T(8,128)S(1)} %maximum_convert_fusion) | copy-start | bytes 19206148
  39.0 8.8 %copy-start.1 = (f32[1,4,512,768]{3,2,1,0:T(8,128)}, f32[1,4,512,768]{3,2,1,0:T(8,128)S(1)}, u32[]{:S(2)}) copy-start(f32[1,4,512,768]{3,2,1,0:T(8,128)S(1)} %get-tuple-element.62) | copy-start | bytes 18874372
  39.0 8.8 %copy-start.2 = (f32[1,4,512,768]{3,2,1,0:T(8,128)}, f32[1,4,512,768]{3,2,1,0:T(8,128)S(1)}, u32[]{:S(2)}) copy-start(f32[1,4,512,768]{3,2,1,0:T(8,128)S(1)} %get-tuple-element.63) | copy-start | bytes 18874372
  47.8 17.0 %copy-start.3 = (f32[1,4,512,768]{3,2,1,0:T(8,128)}, f32[1,4,512,768]{3,2,1,0:T(8,128)S(1)}, u32[]{:S(2)}) copy-start(f32[1,4,512,768]{3,2,1,0:T(8,128)S(1)} %get-tuple-element.60) | copy-start | bytes 18874372
  90.6 41.3 %slice-start = ((s8[6488064]{0:T(1024)(128)(4,1)}), s8[4194304]{0:T(1024)(128)(4,1)S(1)}, s32[]{:S(2)}) async-start(s8[6488064]{0:T(1024)(128)(4,1)} %bitcast.78), calls=%async_computation | async-start | bytes 8388608
  111.3 20.6 %slice-start.1 = ((s8[6488064]{0:T(1024)(128)(4,1)}), s8[2293760]{0:T(1024)(128)(4,1)S(1)}, s32[]{:S(2)}) async-start(s8[6488064]{0:T(1024)(128)(4,1)} %bitcast.78), calls=%async_computation.1 | async-start | bytes 4587520
  184.4 59.4 %copy-start.5 = (f32[6,768]{1,0:T(8,128)S(1)}, f32[6,768]{1,0:T(8,128)}, u32[]{:S(2)}) copy-start(f32[6,768]{1,0:T(8,128)} %param.8) | copy-start | bytes 55300
  184.4 59.4 %copy-start.6 = (f32[6,768]{1,0:T(8,128)S(1)}, f32[6,768]{1,0:T(8,128)}, u32[]{:S(2)}) copy-start(f32[6,768]{1,0:T(8,128)} %param.9) | copy-start | bytes 55300
  184.4 59.4 %copy-start.7 = (f32[6,768]{1,0:T(8,128)S(1)}, f32[6,768]{1,0:T(8,128)}, u32[]{:S(2)}) copy-start(f32[6,768]{1,0:T(8,128)} %param.10) | copy-start | bytes 55300
  239.5 5.0 %collective-permute-start.3 = (bf16[4,3,768]{2,1,0:T(4,128)(2,1)S(1)}, bf16[4,3,768]{2,1,0:T(4,128)(2,1)S(1)}, u32[]{:S(2)}, u32[]{:S(2)}) collective-permute-start(bf16[4,3,768]{2,1,0:T(4,128)(2,1)S(1)} %slice.128), channel_id=1, source_target_pairs={{0,1},{1,2},{2,3},{4,5},{5,6},{6,7},{8,9},{9,10},{10,11},{12,13},{... | collective-permute-start | bytes 55304 | tf_op jit(solution)/shard_map/ppermute | solution.py:23
  241.4 5.4 %collective-permute-start.2 = (bf16[4,6,768]{2,1,0:T(8,128)(2,1)S(1)}, bf16[4,6,768]{2,1,0:T(8,128)(2,1)S(1)}, u32[]{:S(2)}, u32[]{:S(2)}) collective-permute-start(bf16[4,6,768]{2,1,0:T(8,128)(2,1)S(1)} %slice.127), channel_id=1, source_target_pairs={{1,0},{2,1},{3,2},{5,4},{6,5},{7,6},{9,8},{10,9},{11,10},{13,12},{... | collective-permute-start | bytes 110600 | tf_op jit(solution)/shard_map/ppermute | solution.py:23
